TPU v7x, 128 devices: a whole 4x4x4 slice. The times are simulated.
128 devices in a mesh: aux: 16 (over z, x_lo, core), rows: 8 (over y, x_hi).
Axes of the slice: x: 4 (x_hi: 2, x_lo: 2; x = x_hi * 2 + x_lo), y: 4, z: 4, core: 2. Of those that a mesh axis runs over, the one named last changes fastest.
Arguments:
- three_center: bfloat16 [128, 40, 16, 128, 128], P('aux', 'rows'), may hold values from -6 to 6
- coeffs: bfloat16 [16384, 128], P('aux'), may hold values from -0.01171875 to 0.01171875
- sig_blocks: int32 [40, 16], P('rows'), may hold values from 0 to 7
- k_columns: int32 [40, 12], P('rows'), may hold values from 0 to 39, as said below
- owners: int32 [480, 1], P('rows'), may hold values from 0 to 7; in each aligned block of 60 rows (0 to 59, 60 to 119, ...) at most 15 rows name the same one
Outputs:
- exchange_blocks: float32 [960, 128, 128], P('rows', 'aux')
Inputs may be any that keep to these rules, and one draw needn't show every extreme that they name: `owners`: among the 60 entries of one rows index, no owner is named more than 15 times. `k_columns`: the 12 entries of one row block are distinct, and the first entry of row block m is m itself.
All inputs are finite; a program needn't handle non-finite values.
Results may differ from a plain program's by a relative error of at most 0.0014.
Values may be sent and summed in bfloat16 or wider, within the bound.
A program may use at most 128 MiB of HBM per device.

v0:
```python
import jax
import jax.numpy as jnp
from jax import lax
from jax.sharding import PartitionSpec as P

BS = 128
OCC = 128
BLK_DEV = 8
CAP = 15


def bucket(values, owner_ids, owner_total, capacity):
    onehot = (owner_ids[:, None] == jnp.arange(owner_total, dtype=jnp.int32)[None, :]).astype(
        jnp.int32
    )
    ranks = jnp.sum(jnp.cumsum(onehot, axis=0) * onehot, axis=1) - 1
    target = owner_ids * capacity + ranks
    buffer = jnp.zeros((owner_total * capacity,) + values.shape[1:], values.dtype)
    return buffer.at[target].set(values)


def per_device(three_center, coeffs, sig_blocks, k_columns, owners):
    row_local = three_center.shape[1]
    owner_count = three_center.shape[2]
    panels = lax.all_gather(coeffs, "aux", axis=0, tiled=True)
    blocks = panels.reshape(owner_count * BLK_DEV, BS, OCC)
    wanted = sig_blocks + (jnp.arange(owner_count, dtype=jnp.int32) * BLK_DEV)[None, :]
    picked = blocks[wanted]
    half_sum = jnp.einsum(
        "pmqab,mqbo->pmao", three_center, picked, preferred_element_type=jnp.float32
    )
    half = half_sum.astype(jnp.bfloat16)
    every_row = lax.all_gather(half, "rows", axis=1, tiled=True)
    pieces_list = []
    for index in range(row_local):
        partners = jnp.take(every_row, k_columns[index], axis=1)
        pieces_list.append(
            jnp.einsum(
                "pai,psbi->sab", half[:, index], partners, preferred_element_type=jnp.float32
            )
        )
    partial_value = jnp.concatenate(pieces_list, axis=0)
    owner_total = lax.axis_size("rows")
    owner_ids = owners[:, 0]
    reduced = lax.psum_scatter(partial_value, "aux", scatter_dimension=1, tiled=True)
    buffer = bucket(reduced, owner_ids, owner_total, CAP)
    buffer = buffer.reshape(owner_total, CAP, reduced.shape[1], BS)
    arrived = lax.all_to_all(buffer, "rows", split_axis=0, concat_axis=0, tiled=True)
    return arrived.reshape(owner_total * CAP, reduced.shape[1], BS)


def solution(mesh):
    return jax.shard_map(
        per_device,
        mesh=mesh,
        in_specs=(
            P("aux", "rows", None, None, None),
            P("aux", None),
            P("rows", None),
            P("rows", None),
            P("rows", None),
        ),
        out_specs=P("rows", "aux", None),
        check_vma=False,
    )
```

profile of v0, /device:TPU:0, one launch (start us, length us, event | category | flops | bytes accessed | tf_op | source)
XLA Modules:
  0.0 333.1 jit_solution(17910618142357279781)
XLA Ops:
  6.5 0.7 all-gather.3.cloned.1.call-update
  7.3 0.0 all-gather.5.cloned.1.call-start
  7.3 0.7 compare_select_fusion
  8.0 0.1 reshape.72
  8.1 40.8 %all-gather.3.cloned.1.call-done = bf16[16384,128]{1,0:T(8,128)(2,1)} async-done(((bf16[1024,128]{1,0:T(8,128)(2,1)}), bf16[16384,128]{1,0:T(8,128)(2,1)}) %all-gather.3.cloned.1.call-update) | async-done | bytes 4194320 | tf_op jit(solution)/shard_map/all_gather | solution.py:25
  48.9 3.2 gather_fusion
  52.1 12.0 %fusion.29 = bf16[8,5,128,128]{2,3,0,1:T(8,128)(2,1)} fusion(bf16[5,16,128,128,1]{3,2,1,4,0:T(8,128)(2,1)S(1)} %bitcast.135, bf16[8,5,16,128,128]{4,3,2,1,0:T(8,128)(2,1)} %param.7), kind=kOutput, calls=%fused_computation.35 | convolution fusion | flops 2685009920 | bytes 24903680 | tf_op jit(solution)/shard_map/pmqab,mqbo->pmao/dot_general | solution.py:29
  64.1 2.4 copy.33
  66.6 0.0 all-gather.5.cloned.1.call-update
  66.6 0.0 reduce-scatter.2.cloned.1.call-start
  66.7 125.3 %all-gather.5.cloned.1.call-done = bf16[8,40,128,128]{3,2,0,1:T(8,128)(2,1)} async-done(((bf16[8,5,128,128]{3,2,0,1:T(8,128)(2,1)}), bf16[8,40,128,128]{3,2,0,1:T(8,128)(2,1)}) %all-gather.5.cloned.1.call-update) | async-done | bytes 10485776 | tf_op jit(solution)/shard_map/all_gather | solution.py:33
  192.0 5.1 %gather_fusion.1 = bf16[12,8,128,128]{3,2,1,0:T(8,128)(2,1)S(1)} fusion(bf16[8,40,128,128]{3,2,0,1:T(8,128)(2,1)} %all-gather.5.cloned.1.call-done, s32[1024]{0:T(1024)S(1)} %pad_clamp_fusion.4), kind=kCustom, calls=%fused_computation.clone | custom fusion | bytes 6291504 | tf_op jit(solution)/shard_map/jit(_take)/gather | solution.py:36
  197.2 2.9 fusion.35
  200.0 5.1 %gather_fusion.2 = bf16[12,8,128,128]{3,2,1,0:T(8,128)(2,1)S(1)} fusion(bf16[8,40,128,128]{3,2,0,1:T(8,128)(2,1)} %all-gather.5.cloned.1.call-done, s32[1024]{0:T(1024)S(1)} %get-tuple-element.27), kind=kCustom, calls=%fused_computation.1.clone | custom fusion | bytes 6291504 | tf_op jit(solution)/shard_map/jit(_take)/gather | solution.py:36
  205.2 2.8 fusion.41
  208.0 5.1 %gather_fusion.3 = bf16[12,8,128,128]{3,2,1,0:T(8,128)(2,1)S(1)} fusion(bf16[8,40,128,128]{3,2,0,1:T(8,128)(2,1)} %all-gather.5.cloned.1.call-done, s32[1024]{0:T(1024)S(1)} %get-tuple-element.26), kind=kCustom, calls=%fused_computation.2.clone | custom fusion | bytes 6291504 | tf_op jit(solution)/shard_map/jit(_take)/gather | solution.py:36
  213.1 2.9 fusion.47
  216.0 5.1 %gather_fusion.4 = bf16[12,8,128,128]{3,2,1,0:T(8,128)(2,1)S(1)} fusion(bf16[8,40,128,128]{3,2,0,1:T(8,128)(2,1)} %all-gather.5.cloned.1.call-done, s32[1024]{0:T(1024)S(1)} %get-tuple-element.25), kind=kCustom, calls=%fused_computation.3.clone | custom fusion | bytes 6291504 | tf_op jit(solution)/shard_map/jit(_take)/gather | solution.py:36
  221.1 2.9 fusion.53
  224.1 5.1 %gather_fusion.5 = bf16[12,8,128,128]{3,2,1,0:T(8,128)(2,1)S(1)} fusion(bf16[8,40,128,128]{3,2,0,1:T(8,128)(2,1)} %all-gather.5.cloned.1.call-done, s32[1024]{0:T(1024)S(1)} %get-tuple-element.24), kind=kCustom, calls=%fused_computation.4.clone | custom fusion | bytes 6291504 | tf_op jit(solution)/shard_map/jit(_take)/gather | solution.py:36
  229.2 2.9 fusion.59
  232.1 5.1 %copy.39 = f32[60,128,128]{2,0,1:T(8,128)} copy(f32[60,128,128]{1,2,0:T(8,128)} %fusion.59) | data formatting | bytes 7864320 | tf_op jit(solution)/shard_map/concatenate | solution.py:42
  237.2 0.0 reduce-scatter.2.cloned.1.call-update
  237.2 0.6 copy-done
  237.8 0.1 fusion.62
  237.9 0.1 reduce_window_sum.11
  238.0 0.2 select_reduce_fusion
  238.2 67.7 %reduce-scatter.2.cloned.1.call-done = f32[60,8,128]{2,0,1:T(8,128)} async-done(((f32[60,128,128]{2,0,1:T(8,128)}), f32[60,8,128]{2,0,1:T(8,128)}) %reduce-scatter.2.cloned.1.call-update) | async-done | bytes 245776 | tf_op jit(solution)/shard_map/reduce_scatter | solution.py:45
  305.9 1.1 copy.40
  307.1 2.5 scatter_fusion
  309.6 16.2 %all_to_all.5 = f32[8,15,8,128]{3,2,1,0:T(8,128)S(1)} all-to-all(f32[8,15,8,128]{3,2,1,0:T(8,128)S(1)} %bitcast.134), channel_id=1, replica_groups=mesh['aux'=16,'rows'=8] {'rows'}, dimensions={0} | all-to-all | bytes 983040 | tf_op jit(solution)/shard_map/all_to_all | solution.py:48
  325.8 0.8 copy.70
  (12 shorter events, 0.1 us)
Async XLA Ops:
  6.5 42.4 %all-gather.3.cloned.1.call-start = ((), (), s32[]{:S(2)}) async-start(), calls=%async_computation.2 | async-start | bytes 4456448 | tf_op jit(solution)/shard_map/all_gather | solution.py:25
  7.3 184.8 %all-gather.5.cloned.1.call-start = ((), (), s32[]{:S(2)}) async-start(), calls=%async_computation.3 | async-start | bytes 11796480 | tf_op jit(solution)/shard_map/all_gather | solution.py:33
  64.1 2.5 copy-start.1
  66.6 239.3 %reduce-scatter.2.cloned.1.call-start = ((), (), s32[]{:S(2)}) async-start(), calls=%async_computation.4 | async-start | bytes 4456448 | tf_op jit(solution)/shard_map/reduce_scatter | solution.py:45
  237.2 0.7 copy-start
Sparse Core Ops, SparseCore 0:
  9.0 39.8 all-gather.2
  66.7 125.2 all-gather.4
  237.3 68.5 reduce-scatter.1
where the time goes:
time: 334 us; the launch traced here: 333 us
  waiting for transfers between devices  235 us (70%)
  local copies, waits for them, and re-layouts  41.5 us (12%)
  matrix products  26.4 us (8%)
  blocking collectives  16.2 us (5%)
  between operations  13.2 us (4%)
    all_gather x1, waiting for transfers between devices, per_device(): every_row = lax.all_gather(half, 'rows', axis=1, tiled=True)  125 us
    reduce_scatter x1, waiting for transfers between devices, per_device(): lax.psum_scatter(partial_value, 'aux', scatter_dimension=1, tiled=True)  67.7 us
    all_gather x1, waiting for transfers between devices, per_device(): panels = lax.all_gather(coeffs, 'aux', axis=0, tiled=True)  40.8 us
    gather x5, local copies, waits for them, and re-layouts, per_device(): partners = jnp.take(every_row, k_columns[index], axis=1)  25.6 us
    all_to_all x1, blocking collectives, per_device(): lax.all_to_all(buffer, 'rows', split_axis=0, concat_axis=0, tiled=True)  16.2 us
    dot_general x5, matrix products, per_device(): jnp.einsum('pai,psbi->sab', half[:, index], partners, preferred_element_t...  14.4 us
    dot_general x1, matrix products, per_device(): jnp.einsum('pmqab,mqbo->pmao', three_center, picked, preferred_element_ty...  12 us
  transfers between devices with their start and end apart: 3, of which 3 were waited for; matrix products, arithmetic and copies ran while one was open for 0% of the time, Pallas kernels for 0%

commit v1 on v0

--- a/solution.py
+++ b/solution.py
@@ -22,7 +22,8 @@
 def per_device(three_center, coeffs, sig_blocks, k_columns, owners):
     row_local = three_center.shape[1]
     owner_count = three_center.shape[2]
-    panels = lax.all_gather(coeffs, "aux", axis=0, tiled=True)
+    sent = jnp.stack([coeffs] * lax.axis_size("aux"))
+    panels = jnp.concatenate(lax.all_to_all(sent, "aux", 0, 0), axis=0)
     blocks = panels.reshape(owner_count * BLK_DEV, BS, OCC)
     wanted = sig_blocks + (jnp.arange(owner_count, dtype=jnp.int32) * BLK_DEV)[None, :]
     picked = blocks[wanted]

time: 334 us -> 352 us (1.054)
  waiting for transfers between devices: 235 us -> 243 us
  starting transfers between devices: 0.08 us -> 6.9 us
  local copies, waits for them, and re-layouts: 41.5 us -> 45.3 us
    all_to_all x0 -> x1, waiting for transfers between devices: none -> 50.2 us  [per_device(): panels = jnp.concatenate(lax.all_to_all(sent, 'aux', 0, 0), axis=0)]
    all_gather x1 -> x0, waiting for transfers between devices: 40.8 us -> none  [per_device(): panels = lax.all_gather(coeffs, 'aux', axis=0, tiled=True)]
    all_to_all x0 -> x1, starting transfers between devices: none -> 6.64 us  [per_device(): panels = jnp.concatenate(lax.all_to_all(sent, 'aux', 0, 0), axis=0)]
    another operation x0 -> x1, local copies, waits for them, and re-layouts: none -> 3.73 us  [per_device(): sent = jnp.stack([coeffs] * lax.axis_size('aux'))]
where the time goes in v1:
time: 352 us; the launch traced here: 351 us
  waiting for transfers between devices  243 us (69%)
  local copies, waits for them, and re-layouts  45.3 us (13%)
  matrix products  26.3 us (7%)
  blocking collectives  16.2 us (5%)
  between operations  13.6 us (4%)
  starting transfers between devices  6.9 us (2%)
    all_gather x1, waiting for transfers between devices, per_device(): every_row = lax.all_gather(half, 'rows', axis=1, tiled=True)  125 us
    reduce_scatter x1, waiting for transfers between devices, per_device(): lax.psum_scatter(partial_value, 'aux', scatter_dimension=1, tiled=True)  67.7 us
    all_to_all x1, waiting for transfers between devices, per_device(): panels = jnp.concatenate(lax.all_to_all(sent, 'aux', 0, 0), axis=0)  50.2 us
    gather x5, local copies, waits for them, and re-layouts, per_device(): partners = jnp.take(every_row, k_columns[index], axis=1)  25.6 us
    all_to_all x1, blocking collectives, per_device(): lax.all_to_all(buffer, 'rows', split_axis=0, concat_axis=0, tiled=True)  16.2 us
    dot_general x5, matrix products, per_device(): jnp.einsum('pai,psbi->sab', half[:, index], partners, preferred_element_t...  14.3 us
    dot_general x1, matrix products, per_device(): jnp.einsum('pmqab,mqbo->pmao', three_center, picked, preferred_element_ty...  12 us
  transfers between devices with their start and end apart: 3, of which 3 were waited for; matrix products, arithmetic and copies ran while one was open for 0% of the time, Pallas kernels for 0%

profile of v1, /device:TPU:0, one launch (start us, length us, event | category | flops | bytes accessed | tf_op | source)
XLA Modules:
  0.0 351.3 jit_solution(7077086093806445569)
XLA Ops:
  6.5 3.7 %stack.2 = bf16[16,1024,128]{2,1,0:T(8,128)(2,1)} broadcast(bf16[1024,128]{1,0:T(8,128)(2,1)} %param.8), dimensions={1,2} | broadcast | bytes 4456448 | tf_op jit(solution)/shard_map/stack | solution.py:25
  10.3 6.6 %all-to-all-start = ((bf16[16,1024,128]{2,1,0:T(8,128)(2,1)}), bf16[16,1024,128]{2,1,0:T(8,128)(2,1)}, u32[]{:S(2)}, u32[]{:S(2)}) async-start(bf16[16,1024,128]{2,1,0:T(8,128)(2,1)} %stack.2), calls=%async_computation | async-start | bytes 8388608 | tf_op jit(solution)/shard_map/all_to_all | solution.py:26
  16.9 0.0 all-gather.2.cloned.1.call-start
  17.0 0.1 reshape.70
  17.1 50.2 %all-to-all-done = bf16[16,1024,128]{2,1,0:T(8,128)(2,1)} async-done(((bf16[16,1024,128]{2,1,0:T(8,128)(2,1)}), bf16[16,1024,128]{2,1,0:T(8,128)(2,1)}, u32[]{:S(2)}, u32[]{:S(2)}) %all-to-all-start) | async-done | bytes 4194336 | tf_op jit(solution)/shard_map/all_to_all | solution.py:26
  67.2 3.2 gather_fusion
  70.5 12.0 %fusion.29 = bf16[8,5,128,128]{2,3,0,1:T(8,128)(2,1)} fusion(bf16[5,16,128,128,1]{3,2,1,4,0:T(8,128)(2,1)S(1)} %bitcast.134, bf16[8,5,16,128,128]{4,3,2,1,0:T(8,128)(2,1)} %param.7), kind=kOutput, calls=%fused_computation.35 | convolution fusion | flops 2685009920 | bytes 24903680 | tf_op jit(solution)/shard_map/pmqab,mqbo->pmao/dot_general | solution.py:30
  82.5 2.4 copy.32
  84.9 0.0 all-gather.2.cloned.1.call-update
  85.0 0.2 reduce-scatter.2.cloned.1.call-start
  85.3 124.8 %all-gather.2.cloned.1.call-done = bf16[8,40,128,128]{3,2,0,1:T(8,128)(2,1)} async-done(((bf16[8,5,128,128]{3,2,0,1:T(8,128)(2,1)}), bf16[8,40,128,128]{3,2,0,1:T(8,128)(2,1)}) %all-gather.2.cloned.1.call-update) | async-done | bytes 10485776 | tf_op jit(solution)/shard_map/all_gather | solution.py:34
  210.1 5.1 %gather_fusion.1 = bf16[12,8,128,128]{3,2,1,0:T(8,128)(2,1)S(1)} fusion(bf16[8,40,128,128]{3,2,0,1:T(8,128)(2,1)} %all-gather.2.cloned.1.call-done, s32[1024]{0:T(1024)S(1)} %pad_clamp_fusion.4), kind=kCustom, calls=%fused_computation.clone | custom fusion | bytes 6291504 | tf_op jit(solution)/shard_map/jit(_take)/gather | solution.py:37
  215.2 2.8 fusion.35
  218.0 5.1 %gather_fusion.2 = bf16[12,8,128,128]{3,2,1,0:T(8,128)(2,1)S(1)} fusion(bf16[8,40,128,128]{3,2,0,1:T(8,128)(2,1)} %all-gather.2.cloned.1.call-done, s32[1024]{0:T(1024)S(1)} %get-tuple-element.27), kind=kCustom, calls=%fused_computation.1.clone | custom fusion | bytes 6291504 | tf_op jit(solution)/shard_map/jit(_take)/gather | solution.py:37
  223.2 2.8 fusion.41
  226.0 5.1 %gather_fusion.3 = bf16[12,8,128,128]{3,2,1,0:T(8,128)(2,1)S(1)} fusion(bf16[8,40,128,128]{3,2,0,1:T(8,128)(2,1)} %all-gather.2.cloned.1.call-done, s32[1024]{0:T(1024)S(1)} %get-tuple-element.26), kind=kCustom, calls=%fused_computation.2.clone | custom fusion | bytes 6291504 | tf_op jit(solution)/shard_map/jit(_take)/gather | solution.py:37
  231.2 2.9 fusion.47
  234.0 5.1 %gather_fusion.4 = bf16[12,8,128,128]{3,2,1,0:T(8,128)(2,1)S(1)} fusion(bf16[8,40,128,128]{3,2,0,1:T(8,128)(2,1)} %all-gather.2.cloned.1.call-done, s32[1024]{0:T(1024)S(1)} %get-tuple-element.25), kind=kCustom, calls=%fused_computation.3.clone | custom fusion | bytes 6291504 | tf_op jit(solution)/shard_map/jit(_take)/gather | solution.py:37
  239.2 2.9 fusion.53
  242.1 5.1 %gather_fusion.5 = bf16[12,8,128,128]{3,2,1,0:T(8,128)(2,1)S(1)} fusion(bf16[8,40,128,128]{3,2,0,1:T(8,128)(2,1)} %all-gather.2.cloned.1.call-done, s32[1024]{0:T(1024)S(1)} %get-tuple-element.24), kind=kCustom, calls=%fused_computation.4.clone | custom fusion | bytes 6291504 | tf_op jit(solution)/shard_map/jit(_take)/gather | solution.py:37
  247.2 2.9 fusion.59
  250.1 5.1 %copy.38 = f32[60,128,128]{2,0,1:T(8,128)} copy(f32[60,128,128]{1,2,0:T(8,128)} %fusion.59) | data formatting | bytes 7864320 | tf_op jit(solution)/shard_map/concatenate | solution.py:43
  255.2 0.0 reduce-scatter.2.cloned.1.call-update
  255.2 0.6 copy-done.1
  255.9 0.1 fusion.62
  255.9 0.1 reduce_window_sum.11
  256.0 0.2 select_reduce_fusion
  256.2 67.7 %reduce-scatter.2.cloned.1.call-done = f32[60,8,128]{2,0,1:T(8,128)} async-done(((f32[60,128,128]{2,0,1:T(8,128)}), f32[60,8,128]{2,0,1:T(8,128)}) %reduce-scatter.2.cloned.1.call-update) | async-done | bytes 245776 | tf_op jit(solution)/shard_map/reduce_scatter | solution.py:46
  323.9 1.1 copy.39
  325.0 2.5 scatter_fusion
  327.5 16.2 %all_to_all.10 = f32[8,15,8,128]{3,2,1,0:T(8,128)S(1)} all-to-all(f32[8,15,8,128]{3,2,1,0:T(8,128)S(1)} %bitcast.133), channel_id=1, replica_groups=mesh['aux'=16,'rows'=8] {'rows'}, dimensions={0} | all-to-all | bytes 983040 | tf_op jit(solution)/shard_map/all_to_all | solution.py:49
  343.7 0.8 copy.71
  (14 shorter events, 0.1 us)
Async XLA Ops:
  10.3 6.7 %copy-start = (s32[5,16]{1,0:T(8,128)S(1)}, s32[5,16]{1,0:T(8,128)}, u32[]{:S(2)}) copy-start(s32[5,16]{1,0:T(8,128)} %param.9) | copy-start | bytes 964
  10.3 57.0 %all-to-all-start = ((bf16[16,1024,128]{2,1,0:T(8,128)(2,1)}), bf16[16,1024,128]{2,1,0:T(8,128)(2,1)}, u32[]{:S(2)}, u32[]{:S(2)}) async-start(bf16[16,1024,128]{2,1,0:T(8,128)(2,1)} %stack.2), calls=%async_computation | async-start | bytes 8388608 | tf_op jit(solution)/shard_map/all_to_all | solution.py:26
  16.9 193.1 %all-gather.2.cloned.1.call-start = ((), (), s32[]{:S(2)}) async-start(), calls=%async_computation.3 | async-start | bytes 11796480 | tf_op jit(solution)/shard_map/all_gather | solution.py:34
  82.5 2.7 copy-start.2
  85.0 238.9 %reduce-scatter.2.cloned.1.call-start = ((), (), s32[]{:S(2)}) async-start(), calls=%async_computation.4 | async-start | bytes 4456448 | tf_op jit(solution)/shard_map/reduce_scatter | solution.py:46
  255.2 0.7 copy-start.1
Sparse Core Ops, SparseCore 0:
  85.1 124.9 all-gather.1
  255.3 68.5 reduce-scatter.1
